TPU v7x, 128 devices: a whole 4x4x4 slice. The times are simulated.
128 devices in a mesh: row: 32 (over x_hi, z, y), ch: 4 (over x_lo, core).
Axes of the slice: x: 4 (x_hi: 2, x_lo: 2; x = x_hi * 2 + x_lo), y: 4, z: 4, core: 2. Of those that a mesh axis runs over, the one named last changes fastest.
Arguments:
- pair_rep: float32 [256, 256, 128], P(('row', 'ch')), may hold values from -6 to 6
- pair_mask: int32 [256, 256], P(('row', 'ch')), may hold values from 0 to 1, as said below
- ln_in_gain: float32 [128], replicated, may hold values from 0.5 to 1.5
- ln_in_bias: float32 [128], replicated, may hold values from -3 to 3
- w_in: float32 [128, 640], replicated, may hold values from -0.5 to 0.5
- b_in: float32 [640], replicated, may hold values from -3 to 3
- ln_out_gain: float32 [128], replicated, may hold values from 0.5 to 1.5
- ln_out_bias: float32 [128], replicated, may hold values from -3 to 3
- w_out: float32 [128, 128], replicated, may hold values from -0.5 to 0.5
- b_out: float32 [128], replicated, may hold values from -3 to 3
- cotangent: float32 [256, 256, 128], P(('row', 'ch')), may hold values from -6 to 6
Outputs:
- update: float32 [256, 256, 128], P(('row', 'ch'))
- grad_pair: float32 [256, 256, 128], P(('row', 'ch'))
- grad_w_in: float32 [128, 640], replicated
- grad_w_out: float32 [128, 128], replicated
Inputs may be any that keep to these rules, and one draw needn't show every extreme that they name: pair_mask[i, k] = m_i m_k, where m is 1 for the residues present in the crop and 0 otherwise.
All inputs are finite; a program needn't handle non-finite values.
Results may differ from a plain program's by a relative error of at most 0.00009.
Values sent between devices are 32-bit elements; how exact they have to be, the bound alone decides.
No kernel may reach another device: no remote copies, remote signals or barrier semaphores. Data moves between devices by JAX's collectives and lax.ppermute only.
A program may use at most 64 MiB of HBM per device.

v0:
```python
import jax
import jax.numpy as jnp
from jax import lax
from jax.sharding import PartitionSpec as P

epsilon = 1e-05


def side_by_side(arrays, axis, split_dim, concat_dim, along):
    ends, at = ([], 0)
    for a in arrays[:-1]:
        at += a.shape[along]
        ends.append(at)
    both = jnp.concatenate(arrays, axis=along)
    return tuple(
        jnp.split(
            lax.all_to_all(both, axis, split_axis=split_dim, concat_axis=concat_dim, tiled=True),
            ends,
            axis=along,
        )
    )


def prelude(field, keep_mask, norm_gain, norm_bias, weights, offsets):
    channels = field.shape[-1]
    hidden = (weights.shape[1] - channels) // 4
    center = jnp.mean(field, -1, keepdims=True)
    spread = jnp.mean((field - center) ** 2, -1, keepdims=True)
    normed = (field - center) * lax.rsqrt(spread + epsilon) * norm_gain + norm_bias
    pieces = jnp.einsum(
        "ikc,cf->fik", normed, weights[:, : 4 * hidden], precision=lax.Precision.HIGHEST
    )
    pieces = pieces + offsets[: 4 * hidden, None, None]
    gate = jax.nn.sigmoid(
        jnp.einsum("ikc,cf->ikf", normed, weights[:, 4 * hidden :], precision=lax.Precision.HIGHEST)
        + offsets[4 * hidden :]
    )
    keep = keep_mask.astype(field.dtype)[None]
    left = keep * jax.nn.sigmoid(pieces[:hidden]) * pieces[hidden : 2 * hidden]
    right = keep * jax.nn.sigmoid(pieces[2 * hidden : 3 * hidden]) * pieces[3 * hidden :]
    return (left, right, gate)


def epilogue(product, gate, norm_gain, norm_bias, weights, offset):
    center = jnp.mean(product, 0, keepdims=True)
    spread = jnp.mean((product - center) ** 2, 0, keepdims=True)
    normed = (product - center) * lax.rsqrt(spread + epsilon) * norm_gain[
        :, None, None
    ] + norm_bias[:, None, None]
    projected = jnp.einsum("hij,hc->ijc", normed, weights, precision=lax.Precision.HIGHEST) + offset
    return gate * projected


def on_device(
    pair_rep,
    pair_mask,
    ln_in_gain,
    ln_in_bias,
    w_in,
    b_in,
    ln_out_gain,
    ln_out_bias,
    w_out,
    b_out,
    cotangent,
):
    row_count = pair_rep.shape[0]
    length = pair_rep.shape[1]
    hidden = w_out.shape[0]
    per_device = hidden // (lax.axis_size("row") * lax.axis_size("ch"))

    def local_prelude(field, weights):
        return prelude(field, pair_mask, ln_in_gain, ln_in_bias, weights, b_in)

    (left_rows, right_rows, gate), prelude_back = jax.vjp(local_prelude, pair_rep, w_in)
    row_shape = (hidden, 1, row_count, length)
    left_cols, right_cols = side_by_side(
        (left_rows.reshape(row_shape), right_rows.reshape(row_shape)), ("row", "ch"), 0, 2, 1
    )
    left_cols = left_cols.reshape(per_device, length, length)
    right_cols = right_cols.reshape(per_device, length, length)
    product = jnp.einsum("hik,hjk->hij", left_cols, right_cols, precision=lax.Precision.HIGHEST)
    product_rows = lax.all_to_all(
        product.reshape(per_device, 1, length, length),
        ("row", "ch"),
        split_axis=2,
        concat_axis=0,
        tiled=True,
    )
    product_rows = product_rows.reshape(hidden, row_count, length)

    def local_epilogue(prod_part, gate_part, weights):
        return epilogue(prod_part, gate_part, ln_out_gain, ln_out_bias, weights, b_out)

    update, epilogue_back = jax.vjp(local_epilogue, product_rows, gate, w_out)
    d_product, d_gate, d_wout = epilogue_back(cotangent)
    d_cols = lax.all_to_all(
        d_product.reshape(row_shape), ("row", "ch"), split_axis=0, concat_axis=2, tiled=True
    )
    d_cols = d_cols.reshape(per_device, length, length)
    d_left = jnp.einsum("hij,hjk->hik", d_cols, right_cols, precision=lax.Precision.HIGHEST)
    d_right = jnp.einsum("hij,hik->hjk", d_cols, left_cols, precision=lax.Precision.HIGHEST)
    col_shape = (per_device, 1, length, length)
    d_left, d_right = side_by_side(
        (d_left.reshape(col_shape), d_right.reshape(col_shape)), ("row", "ch"), 2, 0, 1
    )
    d_left = d_left.reshape(hidden, row_count, length)
    d_right = d_right.reshape(hidden, row_count, length)
    grad_pair, d_win = prelude_back((d_left, d_right, d_gate))
    wide = w_in.shape[1]
    terms = jnp.concatenate([d_win, d_wout], axis=1)
    terms = lax.all_to_all(terms, ("row", "ch"), split_axis=0, concat_axis=0, tiled=True)
    mine = jnp.sum(terms, 0, keepdims=True) / length
    whole = lax.all_to_all(
        jnp.broadcast_to(mine, terms.shape), ("row", "ch"), split_axis=0, concat_axis=0, tiled=True
    )
    return (update, grad_pair, whole[:, :wide], whole[:, wide:])


def solution(mesh):
    placed = (
        P(("row", "ch"), None, None),
        P(("row", "ch"), None),
        P(),
        P(),
        P(),
        P(),
        P(),
        P(),
        P(),
        P(),
        P(("row", "ch"), None, None),
    )
    return jax.shard_map(
        on_device,
        mesh=mesh,
        in_specs=placed,
        out_specs=(P(("row", "ch"), None, None), P(("row", "ch"), None, None), P(), P()),
        check_vma=False,
    )
```

profile of v0, /device:TPU:1, one launch (start us, length us, event | category | flops | bytes accessed | tf_op | source)
XLA Modules:
  0.0 128.7 jit_solution(5223931275819464922)
XLA Ops:
  0.6 0.0 copy-start
  0.6 0.7 convert_element_type.3
  1.4 1.1 copy.61
  2.5 0.0 copy-done.2
  2.5 0.0 copy-start.3
  2.5 0.1 reduce_sum.97
  2.8 0.0 slice-start
  2.8 0.0 copy-start.7
  2.8 0.0 copy-start.10
  2.8 0.7 copy-done.3
  3.5 0.0 copy-done.7
  3.5 1.1 fusion
  4.6 0.2 multiply_bitcast_fusion.1
  4.8 0.3 copy.64
  5.1 24.7 %all_to_all.72 = f32[128,2,2,256]{3,2,1,0:T(2,128)S(1)} all-to-all(f32[128,2,2,256]{3,2,1,0:T(2,128)S(1)} %copy.64), channel_id=1, replica_groups=mesh['row'=32,'ch'=4] {'row','ch'}, dimensions={0} | all-to-all | bytes 1048576 | tf_op jit(solution)/shard_map/all_to_all | solution.py:17
  29.9 0.3 copy.65
  30.1 0.4 fusion.51
  30.5 0.4 convolution_bitcast_fusion.2
  31.0 1.0 copy.66
  31.9 4.9 %all-to-all-start.1 = ((f32[1,1,256,256]{3,1,0,2:T(1,128)}), f32[1,1,256,256]{3,1,0,2:T(1,128)S(1)}, u32[]{:S(2)}, u32[]{:S(2)}) async-start(f32[1,1,256,256]{3,1,0,2:T(1,128)} %copy.66), calls=%async_computation.1 | async-start | bytes 524288 | tf_op jit(solution)/shard_map/all_to_all | solution.py:83
  36.8 0.7 fusion.6
  37.5 10.3 %all-to-all-done.1 = f32[1,1,256,256]{3,1,0,2:T(1,128)S(1)} async-done(((f32[1,1,256,256]{3,1,0,2:T(1,128)}), f32[1,1,256,256]{3,1,0,2:T(1,128)S(1)}, u32[]{:S(2)}, u32[]{:S(2)}) %all-to-all-start.1) | async-done | bytes 262176 | tf_op jit(solution)/shard_map/all_to_all | solution.py:83
  47.8 0.6 reduce.1
  48.4 0.1 reshape.161
  48.6 0.0 copy-start.1
  48.6 0.1 reduce_sum.99
  48.8 0.8 copy-done.1
  49.5 0.4 multiply_reduce_fusion.1
  50.0 0.1 multiply_reduce_fusion.6
  50.1 0.1 add_bitcast_fusion
  50.1 0.2 copy.69
  50.3 15.3 %all_to_all.73 = f32[128,1,2,256]{3,2,1,0:T(2,128)S(1)} all-to-all(f32[128,1,2,256]{3,2,1,0:T(2,128)S(1)} %copy.69), channel_id=1, replica_groups=mesh['row'=32,'ch'=4] {'row','ch'}, dimensions={0} | all-to-all | bytes 524288 | tf_op jit(solution)/shard_map/all_to_all | solution.py:97
  65.6 0.2 reshape.163
  65.8 0.6 convolution_bitcast_fusion
  66.4 0.4 convolution_bitcast_fusion.1
  66.9 1.2 copy.70
  68.1 4.5 %all-to-all-start.3 = ((f32[1,2,256,256]{3,1,0,2:T(2,128)}), f32[1,2,256,256]{3,1,0,2:T(2,128)S(1)}, u32[]{:S(2)}, u32[]{:S(2)}) async-start(f32[1,2,256,256]{3,1,0,2:T(2,128)} %copy.70), calls=%async_computation.3 | async-start | bytes 1048576 | tf_op jit(solution)/shard_map/all_to_all | solution.py:17
  72.6 0.0 copy-start.13
  72.6 1.3 convolution_bitcast_fusion.4
  73.9 1.4 %fusion.52 = (f32[2,256,128]{2,1,0:T(8,128)}, f32[2,256,128]{2,1,0:T(8,128)S(1)}) fusion(f32[2,256,128]{2,1,0:T(8,128)S(1)} %fusion.6, f32[128]{0:T(128)S(1)} %copy-done.13, f32[128,128]{1,0:T(8,128)S(1)} %copy-done, f32[128]{0:T(128)S(1)} %copy-done.12, f32[128]{0:T(128)S(1)} %copy-done.9, f32[2,256]{1,0:T(2,128)S(1)} %get-tuple-element.33, ...), kind=kOutput, calls=%fused_computation.98 | convolution fusion | flops 101056512 | bytes 1119744 | tf_op jit(solution)/shard_map/jvp(hij,hc->ijc)/dot_general | solution.py:50
  75.3 0.6 convolution_bitcast_fusion.5
  75.9 10.1 %all-to-all-done.3 = f32[1,2,256,256]{3,1,0,2:T(2,128)S(1)} async-done(((f32[1,2,256,256]{3,1,0,2:T(2,128)}), f32[1,2,256,256]{3,1,0,2:T(2,128)S(1)}, u32[]{:S(2)}, u32[]{:S(2)}) %all-to-all-start.3) | async-done | bytes 524320 | tf_op jit(solution)/shard_map/all_to_all | solution.py:17
  86.0 0.3 copy.71
  86.3 0.2 fusion.23
  86.5 0.0 copy-start.8
  86.5 0.0 copy-start.11
  86.6 0.6 copy-done.8
  87.2 0.0 copy-done.11
  87.2 1.9 %convolution_bitcast_fusion.3 = f32[128,512]{0,1:T(8,128)S(1)} fusion(f32[128,2,256]{0,2,1:T(8,128)S(1)} %get-tuple-element.25, f32[128,2,256]{0,2,1:T(8,128)S(1)} %get-tuple-element.27, f32[128,2,256]{0,2,1:T(8,128)S(1)} %get-tuple-element.26, f32[128,2,256]{0,2,1:T(8,128)S(1)} %get-tuple-element.24, f32[2,256,128]{1,2,0:T(8,128)S(1)} %copy.61, ...), kind=kOutput, calls=%fused_computation.15 | convolution fusion | flops 403701760 | bytes 1577984 | tf_op jit(solution)/shard_map/transpose(jvp(ikc,cf->fik))/dot_general | solution.py:30
  89.1 1.2 fusion.7
  90.3 0.0 copy-start.5
  90.3 0.8 copy-done.5
  91.2 1.0 copy.78
  92.2 4.9 %all-to-all-start.4 = ((f32[128,1,768]{2,1,0:T(1,128)}), f32[128,1,768]{2,1,0:T(1,128)S(1)}, u32[]{:S(2)}, u32[]{:S(2)}) async-start(f32[128,1,768]{2,1,0:T(1,128)} %copy.78), calls=%async_computation.4 | async-start | bytes 786432 | tf_op jit(solution)/shard_map/all_to_all | solution.py:112
  97.1 0.5 multiply_reduce_fusion.5
  97.6 11.5 %all-to-all-done.4 = f32[128,1,768]{2,1,0:T(1,128)S(1)} async-done(((f32[128,1,768]{2,1,0:T(1,128)}), f32[128,1,768]{2,1,0:T(1,128)S(1)}, u32[]{:S(2)}, u32[]{:S(2)}) %all-to-all-start.4) | async-done | bytes 393248 | tf_op jit(solution)/shard_map/all_to_all | solution.py:112
  109.1 0.3 reduce_sum.125
  109.4 0.9 broadcast_in_dim.8
  110.4 4.8 %all-to-all-start.5 = ((f32[128,1,768]{2,1,0:T(1,128)}), f32[128,1,768]{2,1,0:T(1,128)S(1)}, u32[]{:S(2)}, u32[]{:S(2)}) async-start(f32[128,1,768]{2,1,0:T(1,128)} %broadcast_in_dim.8), calls=%async_computation.5 | async-start | bytes 786432 | tf_op jit(solution)/shard_map/all_to_all | solution.py:114
  115.2 0.1 add_add_fusion
  115.3 0.8 copy.79
  116.1 11.1 %all-to-all-done.5 = f32[128,1,768]{2,1,0:T(1,128)S(1)} async-done(((f32[128,1,768]{2,1,0:T(1,128)}), f32[128,1,768]{2,1,0:T(1,128)S(1)}, u32[]{:S(2)}, u32[]{:S(2)}) %all-to-all-start.5) | async-done | bytes 393248 | tf_op jit(solution)/shard_map/all_to_all | solution.py:114
  127.3 0.6 slice.45
  127.9 0.7 slice.44
  (29 shorter events, 0.3 us)
Async XLA Ops:
  0.6 48.1 %copy-start = (f32[128,128]{1,0:T(8,128)S(1)}, f32[128,128]{1,0:T(8,128)}, u32[]{:S(2)}) copy-start(f32[128,128]{1,0:T(8,128)} %param.19) | copy-start | bytes 196612
  1.4 1.2 copy-start.2
  2.5 1.0 copy-start.3
  2.8 0.8 slice-start
  2.8 0.7 copy-start.7
  2.8 0.7 copy-start.10
  31.9 4.9 %copy-start.6 = (f32[640]{0:T(1024)S(1)}, f32[640]{0:T(1024)}, u32[]{:S(2)}) copy-start(f32[640]{0:T(1024)} %param.16) | copy-start | bytes 7684
  31.9 15.9 %all-to-all-start.1 = ((f32[1,1,256,256]{3,1,0,2:T(1,128)}), f32[1,1,256,256]{3,1,0,2:T(1,128)S(1)}, u32[]{:S(2)}, u32[]{:S(2)}) async-start(f32[1,1,256,256]{3,1,0,2:T(1,128)} %copy.66), calls=%async_computation.1 | async-start | bytes 524288 | tf_op jit(solution)/shard_map/all_to_all | solution.py:83
  48.6 1.0 copy-start.1
  48.7 0.8 copy-start.9
  68.0 4.5 %copy-start.12 = (f32[128]{0:T(128)S(1)}, f32[128]{0:T(128)}, u32[]{:S(2)}) copy-start(f32[128]{0:T(128)} %param.18) | copy-start | bytes 1540
  68.1 18.0 %all-to-all-start.3 = ((f32[1,2,256,256]{3,1,0,2:T(2,128)}), f32[1,2,256,256]{3,1,0,2:T(2,128)S(1)}, u32[]{:S(2)}, u32[]{:S(2)}) async-start(f32[1,2,256,256]{3,1,0,2:T(2,128)} %copy.70), calls=%async_computation.3 | async-start | bytes 1048576 | tf_op jit(solution)/shard_map/all_to_all | solution.py:17
  72.6 1.3 %copy-start.13 = (f32[128]{0:T(128)S(1)}, f32[128]{0:T(128)}, u32[]{:S(2)}) copy-start(f32[128]{0:T(128)} %param.20) | copy-start | bytes 1540
  86.5 0.7 copy-start.8
  86.5 0.7 copy-start.11
  87.2 1.9 %copy-start.4 = (f32[128,640]{1,0:T(8,128)S(1)}, f32[128,640]{1,0:T(8,128)}, u32[]{:S(2)}) copy-start(f32[128,640]{1,0:T(8,128)} %param.15) | copy-start | bytes 983044
  90.3 0.8 copy-start.5
  92.2 16.9 %all-to-all-start.4 = ((f32[128,1,768]{2,1,0:T(1,128)}), f32[128,1,768]{2,1,0:T(1,128)S(1)}, u32[]{:S(2)}, u32[]{:S(2)}) async-start(f32[128,1,768]{2,1,0:T(1,128)} %copy.78), calls=%async_computation.4 | async-start | bytes 786432 | tf_op jit(solution)/shard_map/all_to_all | solution.py:112
  110.4 16.9 %all-to-all-start.5 = ((f32[128,1,768]{2,1,0:T(1,128)}), f32[128,1,768]{2,1,0:T(1,128)S(1)}, u32[]{:S(2)}, u32[]{:S(2)}) async-start(f32[128,1,768]{2,1,0:T(1,128)} %broadcast_in_dim.8), calls=%async_computation.5 | async-start | bytes 786432 | tf_op jit(solution)/shard_map/all_to_all | solution.py:114
where the time goes:
time: 129 us
  waiting for transfers between devices  43 us (33%)
  blocking collectives  40 us (31%)
  starting transfers between devices  19.1 us (15%)
  local copies, waits for them, and re-layouts  12.2 us (9%)
  matrix products  10.4 us (8%)
  other arithmetic  2.76 us (2%)
    all_to_all x1, blocking collectives, side_by_side(): lax.all_to_all(both, axis, split_axis=split_dim, concat_axis=concat_dim,...  24.7 us
    all_to_all x1, blocking collectives, on_device(): lax.all_to_all(d_product.reshape(row_shape), ('row', 'ch'), split_axis=0,...  15.3 us
    all_to_all x1, waiting for transfers between devices, on_device(): lax.all_to_all(terms, ('row', 'ch'), split_axis=0, concat_axis=0, tiled=T...  11.5 us
    all_to_all x1, waiting for transfers between devices, on_device(): lax.all_to_all(jnp.broadcast_to(mine, terms.shape), ('row', 'ch'), split_...  11.1 us
    all_to_all x1, waiting for transfers between devices, on_device(): lax.all_to_all(product.reshape(per_device, 1, length, length), ('row', 'c...  10.3 us
    all_to_all x1, waiting for transfers between devices, side_by_side(): lax.all_to_all(both, axis, split_axis=split_dim, concat_axis=concat_dim,...  10.1 us
    unnamed x31, local copies, waits for them, and re-layouts  5 us
    all_to_all x1, starting transfers between devices, on_device(): lax.all_to_all(product.reshape(per_device, 1, length, length), ('row', 'c...  4.88 us
  transfers between devices with their start and end apart: 4, of which 4 were waited for; matrix products, arithmetic and copies ran while one was open for 4% of the time, Pallas kernels for 0%

commit v1 on v0

--- a/solution.py
+++ b/solution.py
@@ -80,13 +80,12 @@
     left_cols = left_cols.reshape(per_device, length, length)
     right_cols = right_cols.reshape(per_device, length, length)
     product = jnp.einsum("hik,hjk->hij", left_cols, right_cols, precision=lax.Precision.HIGHEST)
-    product_rows = lax.all_to_all(
-        product.reshape(per_device, 1, length, length),
-        ("row", "ch"),
-        split_axis=2,
-        concat_axis=0,
-        tiled=True,
-    )
+    packet = product.reshape(per_device, 1, length, length)
+    before = jax.lax.axis_size(("row", "ch"))
+    even = jnp.split(packet, before, axis=2)
+    piece_out = jnp.stack(even)
+    block_out = jax.lax.all_to_all(piece_out, axis_name=("row", "ch"), split_axis=0, concat_axis=0)
+    product_rows = jnp.concatenate(block_out, axis=0)
     product_rows = product_rows.reshape(hidden, row_count, length)
 
     def local_epilogue(prod_part, gate_part, weights):

time: 129 us -> 202 us (1.57)
  local copies, waits for them, and re-layouts: 12.2 us -> 84.6 us
    unnamed x31 -> x156, local copies, waits for them, and re-layouts: 5 us -> 77.8 us
  transfers between devices with their start and end apart: 4 -> 4, of which waited for: 4 -> 4; matrix products, arithmetic and copies ran while one was open for 4% -> 2% of each run, Pallas kernels for 0% -> 0%
where the time goes in v1:
time: 202 us; the launch traced here: 201 us
  local copies, waits for them, and re-layouts  84.6 us (42%)
  waiting for transfers between devices  43.7 us (22%)
  blocking collectives  40.1 us (20%)
  starting transfers between devices  19.1 us (9%)
  matrix products  9.82 us (5%)
  other arithmetic  2.84 us (1%)
    unnamed x156, local copies, waits for them, and re-layouts  77.8 us
    all_to_all x1, blocking collectives, side_by_side(): lax.all_to_all(both, axis, split_axis=split_dim, concat_axis=concat_dim,...  24.7 us
    all_to_all x1, blocking collectives, on_device(): lax.all_to_all(d_product.reshape(row_shape), ('row', 'ch'), split_axis=0,...  15.3 us
    all_to_all x1, waiting for transfers between devices, on_device(): lax.all_to_all(terms, ('row', 'ch'), split_axis=0, concat_axis=0, tiled=T...  11.5 us
    all_to_all x1, waiting for transfers between devices, on_device(): lax.all_to_all(jnp.broadcast_to(mine, terms.shape), ('row', 'ch'), split_...  11.1 us
    all_to_all x1, waiting for transfers between devices, side_by_side(): lax.all_to_all(both, axis, split_axis=split_dim, concat_axis=concat_dim,...  10.8 us
    all_to_all x1, waiting for transfers between devices, on_device(): jax.lax.all_to_all(piece_out, axis_name=('row', 'ch'), split_axis=0, conc...  10.3 us
    all_to_all x1, starting transfers between devices, on_device(): jax.lax.all_to_all(piece_out, axis_name=('row', 'ch'), split_axis=0, conc...  4.88 us
  transfers between devices with their start and end apart: 4, of which 4 were waited for; matrix products, arithmetic and copies ran while one was open for 2% of the time, Pallas kernels for 0%

profile of v1, /device:TPU:1, one launch (start us, length us, event | category | flops | bytes accessed | tf_op | source)
XLA Modules:
  0.0 201.3 jit_solution(13742376978745176891)
XLA Ops:
  0.6 0.7 convert_element_type.3
  1.4 1.1 copy.4123
  2.8 0.7 copy-done.3
  3.5 1.1 fusion
  5.1 24.7 %all_to_all.68 = f32[128,2,2,256]{3,2,1,0:T(2,128)S(1)} all-to-all(f32[128,2,2,256]{3,2,1,0:T(2,128)S(1)} %copy.4126), channel_id=1, replica_groups=mesh['row'=32,'ch'=4] {'row','ch'}, dimensions={0} | all-to-all | bytes 1048576 | tf_op jit(solution)/shard_map/all_to_all | solution.py:17
  31.0 0.6 constant_dynamic-update-slice_fusion.127
  31.5 0.6 constant_dynamic-update-slice_fusion.126
  32.1 0.6 constant_dynamic-update-slice_fusion.125
  32.7 0.6 constant_dynamic-update-slice_fusion.124
  33.9 0.6 constant_dynamic-update-slice_fusion.122
  34.4 0.6 constant_dynamic-update-slice_fusion.121
  35.0 0.6 constant_dynamic-update-slice_fusion.120
  36.2 0.6 constant_dynamic-update-slice_fusion.118
  36.8 0.6 constant_dynamic-update-slice_fusion.117
  37.3 0.6 constant_dynamic-update-slice_fusion.116
  38.5 0.6 constant_dynamic-update-slice_fusion.114
  39.1 0.6 constant_dynamic-update-slice_fusion.113
  39.7 0.6 constant_dynamic-update-slice_fusion.112
  40.8 0.6 constant_dynamic-update-slice_fusion.110
  41.4 0.6 constant_dynamic-update-slice_fusion.109
  42.0 0.6 constant_dynamic-update-slice_fusion.108
  43.1 0.6 constant_dynamic-update-slice_fusion.106
  43.7 0.6 constant_dynamic-update-slice_fusion.105
  44.3 0.6 constant_dynamic-update-slice_fusion.104
  45.5 0.6 constant_dynamic-update-slice_fusion.102
  46.0 0.6 constant_dynamic-update-slice_fusion.101
  46.6 0.6 constant_dynamic-update-slice_fusion.100
  47.8 0.6 constant_dynamic-update-slice_fusion.98
  48.4 0.6 constant_dynamic-update-slice_fusion.97
  48.9 0.6 constant_dynamic-update-slice_fusion.96
  50.1 0.6 constant_dynamic-update-slice_fusion.94
  50.7 0.6 constant_dynamic-update-slice_fusion.93
  51.3 0.6 constant_dynamic-update-slice_fusion.92
  52.4 0.6 constant_dynamic-update-slice_fusion.90
  53.0 0.6 constant_dynamic-update-slice_fusion.89
  53.6 0.6 constant_dynamic-update-slice_fusion.88
  54.7 0.6 constant_dynamic-update-slice_fusion.86
  55.3 0.6 constant_dynamic-update-slice_fusion.85
  55.9 0.6 constant_dynamic-update-slice_fusion.84
  57.1 0.6 constant_dynamic-update-slice_fusion.82
  105.2 4.9 %all-to-all-start.1 = ((f32[128,1,1,2,256]{4,3,2,1,0:T(2,128)}), f32[128,1,1,2,256]{4,3,2,1,0:T(2,128)S(1)}, u32[]{:S(2)}, u32[]{:S(2)}) async-start(f32[128,1,1,2,256]{4,3,2,1,0:T(2,128)} %constant_dynamic-update-slice_fusion), calls=%async_computation.1 | async-start | bytes 524288 | tf_op jit(solution)/shard_map/all_to_all | solution.py:87
  110.1 0.7 fusion.6
  110.8 10.3 %all-to-all-done.1 = f32[128,1,1,2,256]{4,3,2,1,0:T(2,128)S(1)} async-done(((f32[128,1,1,2,256]{4,3,2,1,0:T(2,128)}), f32[128,1,1,2,256]{4,3,2,1,0:T(2,128)S(1)}, u32[]{:S(2)}, u32[]{:S(2)}) %all-to-all-start.1) | async-done | bytes 262176 | tf_op jit(solution)/shard_map/all_to_all | solution.py:87
  121.4 0.8 copy-done.1
  123.7 15.3 %all_to_all.69 = f32[128,1,2,256]{3,2,1,0:T(2,128)S(1)} all-to-all(f32[128,1,2,256]{3,2,1,0:T(2,128)S(1)} %copy.4130), channel_id=1, replica_groups=mesh['row'=32,'ch'=4] {'row','ch'}, dimensions={0} | all-to-all | bytes 524288 | tf_op jit(solution)/shard_map/all_to_all | solution.py:96
  139.2 0.6 convolution_bitcast_fusion
  140.2 1.2 copy.4131
  141.4 4.5 %all-to-all-start.3 = ((f32[1,2,256,256]{3,1,0,2:T(2,128)}), f32[1,2,256,256]{3,1,0,2:T(2,128)S(1)}, u32[]{:S(2)}, u32[]{:S(2)}) async-start(f32[1,2,256,256]{3,1,0,2:T(2,128)} %copy.4131), calls=%async_computation.3 | async-start | bytes 1048576 | tf_op jit(solution)/shard_map/all_to_all | solution.py:17
  146.0 0.8 convolution_bitcast_fusion.4
  146.8 1.2 fusion.54
  147.9 0.6 convolution_bitcast_fusion.5
  148.6 10.8 %all-to-all-done.3 = f32[1,2,256,256]{3,1,0,2:T(2,128)S(1)} async-done(((f32[1,2,256,256]{3,1,0,2:T(2,128)}), f32[1,2,256,256]{3,1,0,2:T(2,128)S(1)}, u32[]{:S(2)}, u32[]{:S(2)}) %all-to-all-start.3) | async-done | bytes 524320 | tf_op jit(solution)/shard_map/all_to_all | solution.py:17
  159.9 0.6 copy-done.7
  160.6 1.9 convolution_bitcast_fusion.3
  162.5 1.2 fusion.7
  163.7 1.0 copy.4140
  164.8 4.9 %all-to-all-start.4 = ((f32[128,1,768]{2,1,0:T(1,128)}), f32[128,1,768]{2,1,0:T(1,128)S(1)}, u32[]{:S(2)}, u32[]{:S(2)}) async-start(f32[128,1,768]{2,1,0:T(1,128)} %copy.4140), calls=%async_computation.4 | async-start | bytes 786432 | tf_op jit(solution)/shard_map/all_to_all | solution.py:111
  170.2 11.5 %all-to-all-done.4 = f32[128,1,768]{2,1,0:T(1,128)S(1)} async-done(((f32[128,1,768]{2,1,0:T(1,128)}), f32[128,1,768]{2,1,0:T(1,128)S(1)}, u32[]{:S(2)}, u32[]{:S(2)}) %all-to-all-start.4) | async-done | bytes 393248 | tf_op jit(solution)/shard_map/all_to_all | solution.py:111
  182.0 0.9 broadcast_in_dim.8
  182.9 4.8 %all-to-all-start.5 = ((f32[128,1,768]{2,1,0:T(1,128)}), f32[128,1,768]{2,1,0:T(1,128)S(1)}, u32[]{:S(2)}, u32[]{:S(2)}) async-start(f32[128,1,768]{2,1,0:T(1,128)} %broadcast_in_dim.8), calls=%async_computation.5 | async-start | bytes 786432 | tf_op jit(solution)/shard_map/all_to_all | solution.py:113
  187.9 0.8 copy.4141
  188.7 11.1 %all-to-all-done.5 = f32[128,1,768]{2,1,0:T(1,128)S(1)} async-done(((f32[128,1,768]{2,1,0:T(1,128)}), f32[128,1,768]{2,1,0:T(1,128)S(1)}, u32[]{:S(2)}, u32[]{:S(2)}) %all-to-all-start.5) | async-done | bytes 393248 | tf_op jit(solution)/shard_map/all_to_all | solution.py:113
  199.9 0.6 slice.45
  200.5 0.7 slice.44
  (153 shorter events, 59.6 us)
Async XLA Ops:
  0.6 120.8 %copy-start = (f32[128,128]{1,0:T(8,128)S(1)}, f32[128,128]{1,0:T(8,128)}, u32[]{:S(2)}) copy-start(f32[128,128]{1,0:T(8,128)} %param.19) | copy-start | bytes 196612
  1.4 1.2 copy-start.2
  2.5 1.0 copy-start.3
  2.8 0.8 slice-start
  2.8 0.7 copy-start.6
  2.8 0.7 copy-start.9
  105.2 4.9 %copy-start.5 = (f32[640]{0:T(1024)S(1)}, f32[640]{0:T(1024)}, u32[]{:S(2)}) copy-start(f32[640]{0:T(1024)} %param.16) | copy-start | bytes 7684
  105.2 15.9 %all-to-all-start.1 = ((f32[128,1,1,2,256]{4,3,2,1,0:T(2,128)}), f32[128,1,1,2,256]{4,3,2,1,0:T(2,128)S(1)}, u32[]{:S(2)}, u32[]{:S(2)}) async-start(f32[128,1,1,2,256]{4,3,2,1,0:T(2,128)} %constant_dynamic-update-slice_fusion), calls=%async_computation.1 | async-start | bytes 524288 | tf_op jit(solution)/shard_map/all_to_all | solution.py:87
  121.2 1.0 copy-start.1
  121.2 0.9 copy-start.8
  141.4 4.5 %copy-start.11 = (f32[128]{0:T(128)S(1)}, f32[128]{0:T(128)}, u32[]{:S(2)}) copy-start(f32[128]{0:T(128)} %param.18) | copy-start | bytes 1540
  141.4 18.0 %all-to-all-start.3 = ((f32[1,2,256,256]{3,1,0,2:T(2,128)}), f32[1,2,256,256]{3,1,0,2:T(2,128)S(1)}, u32[]{:S(2)}, u32[]{:S(2)}) async-start(f32[1,2,256,256]{3,1,0,2:T(2,128)} %copy.4131), calls=%async_computation.3 | async-start | bytes 1048576 | tf_op jit(solution)/shard_map/all_to_all | solution.py:17
  146.0 0.8 copy-start.12
  159.9 0.7 copy-start.7
  159.9 0.7 copy-start.10
  160.6 1.9 copy-start.4
  164.8 16.9 %all-to-all-start.4 = ((f32[128,1,768]{2,1,0:T(1,128)}), f32[128,1,768]{2,1,0:T(1,128)S(1)}, u32[]{:S(2)}, u32[]{:S(2)}) async-start(f32[128,1,768]{2,1,0:T(1,128)} %copy.4140), calls=%async_computation.4 | async-start | bytes 786432 | tf_op jit(solution)/shard_map/all_to_all | solution.py:111
  182.9 16.9 %all-to-all-start.5 = ((f32[128,1,768]{2,1,0:T(1,128)}), f32[128,1,768]{2,1,0:T(1,128)S(1)}, u32[]{:S(2)}, u32[]{:S(2)}) async-start(f32[128,1,768]{2,1,0:T(1,128)} %broadcast_in_dim.8), calls=%async_computation.5 | async-start | bytes 786432 | tf_op jit(solution)/shard_map/all_to_all | solution.py:113
